TPU v7x, 32 devices: a whole 2x2x4 slice. The times are simulated.
32 devices in a mesh: group: 2 (over x), chan: 16 (over z, y, core).
Axes of the slice: x: 2, y: 2, z: 4, core: 2. Of those that a mesh axis runs over, the one named last changes fastest.
Arguments:
- voltages: bfloat16 [32, 2, 256, 1024], P(('group', 'chan')), parts along dimension 0, may hold values from -6 to 6
- cal_num: float32 [32, 4, 512], P(('group', 'chan')), parts along dimension 0, may hold values from -6 to 6
- cal_weight: float32 [32, 2, 512], P(('group', 'chan')), parts along dimension 0, may hold values from 0.2 to 5
- flags: int32 [32, 512], P(('group', 'chan')), parts along dimension 0, may hold values 0 or 1
- positions: float32 [2, 512], replicated, may hold values from -300 to 300
- directions: float32 [2, 1024], replicated, may hold values from -0.05 to 0.05
- pointing: int32 [2048], P('group'), parts along dimension 0, may hold values from 0 to 1023, each once
Outputs:
- beam_power: bfloat16 [2048, 16, 128], P(('group', 'chan')), parts along dimension 0
- solved_gains: float32 [32, 4, 512], P(('group', 'chan')), parts along dimension 0
There are 2 independent parts, one for each index of `group`. A program takes and returns all parts, laid end to end along the dimension named above; an argument that names none is the same for every part. Nothing has to cross between parts.
Inputs may be any that keep to these rules, and one draw needn't show every extreme that they name: `pointing`: each table direction is named by exactly one beam.
All inputs are finite; a program needn't handle non-finite values. No bound on the sum of `flags` on one device may be relied on, other than what follows from the above.
Results may differ from a plain program's by a relative error of at most 0.004.
Values may be sent and summed in bfloat16 or wider, within the bound.
No kernel may reach another device: no remote copies, remote signals or barrier semaphores. Data moves between devices by JAX's collectives and lax.ppermute only.
A program may use at most 64 MiB of HBM per device.

v0:
```python
import jax
import jax.numpy as jnp
from jax import lax
from jax.sharding import PartitionSpec as P

ITERS = 8
PENALTY = 2.0
RIDGE = 1.0
TWO_PI = 6.283185307179586
HIGHEST = lax.Precision.HIGHEST


def basis_rows(channel_ids, total):
    place = 2.0 * (channel_ids.astype(jnp.float32) + 0.5) / total - 1.0
    return jnp.stack(
        [
            jnp.ones_like(place),
            place,
            0.5 * (3.0 * place * place - 1.0),
            0.5 * (5.0 * place * place * place - 3.0 * place),
        ],
        axis=1,
    )


def invert_small(matrix):
    order = matrix.shape[0]
    unit = jnp.ones_like(matrix[0, 0])
    nothing = jnp.zeros_like(matrix[0, 0])
    left = [[matrix[row, column] for column in range(order)] for row in range(order)]
    right = [
        [unit if row == column else nothing for column in range(order)] for row in range(order)
    ]
    for pivot in range(order):
        factor = 1.0 / left[pivot][pivot]
        left[pivot] = [entry * factor for entry in left[pivot]]
        right[pivot] = [entry * factor for entry in right[pivot]]
        for row in range(order):
            if row != pivot:
                scale = left[row][pivot]
                left[row] = [
                    first - scale * second for first, second in zip(left[row], left[pivot])
                ]
                right[row] = [
                    first - scale * second for first, second in zip(right[row], right[pivot])
                ]
    return jnp.stack([jnp.stack(line, 0) for line in right], 0)


def beam_matrices(fitted, usable, ratio, projected):
    phase = projected * (TWO_PI * ratio)
    cosine = jnp.cos(phase)
    sine = jnp.sin(phase)
    stations = projected.shape[1]
    scale = usable * stations ** (-0.5)
    matrices = []
    for polar in range(2):
        gain_re = (fitted[2 * polar] * scale)[None, :]
        gain_im = (fitted[2 * polar + 1] * scale)[None, :]
        w_re = (gain_re * cosine - gain_im * sine).astype(jnp.bfloat16)
        w_im = (-(gain_re * sine + gain_im * cosine)).astype(jnp.bfloat16)
        upper = jnp.concatenate([w_re, -w_im], axis=1)
        lower = jnp.concatenate([w_im, w_re], axis=1)
        matrices.append(jnp.concatenate([upper, lower], axis=0))
    return matrices


def detect(matrices, volts):
    beams = matrices[0].shape[0] // 2
    total = jnp.zeros((beams, volts.shape[1]), jnp.float32)
    for polar in range(2):
        output = lax.dot_general(
            matrices[polar],
            volts[polar],
            (((1,), (1,)), ((), ())),
            preferred_element_type=jnp.float32,
        )
        total = total + output[:beams] * output[:beams] + output[beams:] * output[beams:]
    return total


def average_pairs(power):
    return ((power[..., 0::2] + power[..., 1::2]) * 0.5).astype(jnp.bfloat16)


def body(voltages, cal_num, cal_weight, flags, positions, directions, pointing):
    local_count = voltages.shape[0]
    devices = lax.axis_size("chan")
    total = local_count * devices
    channel_ids = lax.axis_index("chan") * local_count + jnp.arange(local_count, dtype=jnp.int32)
    basis = basis_rows(channel_ids, total)
    usable = flags.astype(jnp.float32)
    gram = jnp.einsum("ck,cj,cs->kjs", basis, basis, usable, precision=HIGHEST)
    order = basis.shape[1]
    identity = jnp.eye(order, dtype=jnp.float32)[:, :, None]
    weight4 = jnp.repeat(cal_weight, 2, axis=1)
    mask = usable[:, None, :]
    fitted = jnp.zeros(cal_num.shape, jnp.float32)
    dual = jnp.zeros(cal_num.shape, jnp.float32)
    inverse = None
    for sweep in range(ITERS):
        local = (mask * cal_num + PENALTY * (fitted - dual)) / (mask * weight4 + PENALTY)
        numerator = jnp.einsum("ck,cqs->kqs", basis, mask * (local + dual), precision=HIGHEST)
        if sweep == 0:
            gram_all, summed = lax.psum((gram, numerator), "chan")
            inverse = invert_small(gram_all + RIDGE * identity)
        else:
            summed = lax.psum(numerator, "chan")
        coefficients = jnp.einsum("kjs,jqs->kqs", inverse, summed, precision=HIGHEST)
        fitted = jnp.einsum("ck,kqs->cqs", basis, coefficients, precision=HIGHEST)
        dual = dual + mask * (local - fitted)
    table_size = directions.shape[1]
    one_hot = (pointing[:, None] == jnp.arange(table_size, dtype=jnp.int32)[None, :]).astype(
        jnp.float32
    )
    pointed = jnp.dot(one_hot, directions.T, precision=HIGHEST)
    projected = pointed[:, 0:1] * positions[0][None, :] + pointed[:, 1:2] * positions[1][None, :]
    ratio = 1.0 + 0.3 * (channel_ids.astype(jnp.float32) + 0.5) / total
    weights = beam_matrices(fitted[0], usable[0], ratio[0], projected)
    samples = voltages.shape[2]
    half = samples // 2
    pieces = []
    for part_index in range(2):
        start = part_index * half
        powers = [detect(weights, voltages[0, :, start : start + half])]
        pieces.append(
            lax.all_to_all(
                average_pairs(jnp.stack(powers, axis=1)),
                "chan",
                split_axis=0,
                concat_axis=1,
                tiled=True,
            )
        )
    beam_power = jnp.concatenate(pieces, axis=2)
    return (beam_power, fitted)


def solution(mesh):
    return jax.shard_map(
        body,
        mesh=mesh,
        in_specs=(
            P(("group", "chan"), None, None, None),
            P(("group", "chan"), None, None),
            P(("group", "chan"), None, None),
            P(("group", "chan"), None),
            P(),
            P(),
            P("group"),
        ),
        out_specs=(P(("group", "chan"), None, None), P(("group", "chan"), None, None)),
        check_vma=False,
    )
```

profile of v0, /device:TPU:0, one launch (start us, length us, event | category | flops | bytes accessed | tf_op | source)
XLA Modules:
  0.0 697.2 jit_solution(10860283058843665609)
XLA Ops:
  10.4 1.6 broadcast_multiply_fusion.7
  12.1 2.0 fusion
  14.2 94.6 %all-reduce.3.cloned.1.call-done = (f32[4,4,512]{0,1,2:T(4,128)}, f32[4,4,512]{2,1,0:T(4,128)}) async-done(((f32[4,4,512]{0,1,2:T(4,128)}, f32[4,4,512]{2,1,0:T(4,128)}), (f32[4,4,512]{0,1,2:T(4,128)}, f32[4,4,512]{2,1,0:T(4,128)})) %all-reduce.3.cloned.1.call-update) | async-done | bytes 65552 | tf_op jit(solution)/shard_map/psum | solution.py:105
  110.4 3.5 convolution_bitcast_fusion.7
  113.9 0.9 fusion.22
  115.7 70.1 %psum.65 = f32[4,4,512]{0,1,2:T(4,128)S(1)} all-reduce(f32[4,4,512]{0,1,2:T(4,128)S(1)} %broadcast_multiply_fusion.6), channel_id=1, replica_groups=mesh['group'=2,'chan'=16] {'chan'}, use_global_device_ids=true, to_apply=%region_2.0 | all-reduce | flops 8192 | bytes 65536 | tf_op jit(solution)/shard_map/psum | solution.py:108
  185.8 3.5 convolution_bitcast_fusion.6
  191.1 69.2 %psum.66 = f32[4,4,512]{0,1,2:T(4,128)S(1)} all-reduce(f32[4,4,512]{0,1,2:T(4,128)S(1)} %broadcast_multiply_fusion.5), channel_id=1, replica_groups=mesh['group'=2,'chan'=16] {'chan'}, use_global_device_ids=true, to_apply=%region_3.0 | all-reduce | flops 8192 | bytes 65536 | tf_op jit(solution)/shard_map/psum | solution.py:108
  260.3 3.5 convolution_bitcast_fusion.5
  263.8 0.9 fusion.18
  265.6 69.4 %psum.67 = f32[4,4,512]{0,1,2:T(4,128)S(1)} all-reduce(f32[4,4,512]{0,1,2:T(4,128)S(1)} %broadcast_multiply_fusion.4), channel_id=1, replica_groups=mesh['group'=2,'chan'=16] {'chan'}, use_global_device_ids=true, to_apply=%region_4.0 | all-reduce | flops 8192 | bytes 65536 | tf_op jit(solution)/shard_map/psum | solution.py:108
  335.0 3.5 convolution_bitcast_fusion.4
  338.5 0.9 fusion.16
  340.3 69.2 %psum.68 = f32[4,4,512]{0,1,2:T(4,128)S(1)} all-reduce(f32[4,4,512]{0,1,2:T(4,128)S(1)} %broadcast_multiply_fusion.3), channel_id=1, replica_groups=mesh['group'=2,'chan'=16] {'chan'}, use_global_device_ids=true, to_apply=%region_5.0 | all-reduce | flops 8192 | bytes 65536 | tf_op jit(solution)/shard_map/psum | solution.py:108
  409.5 3.5 convolution_bitcast_fusion.3
  414.8 69.6 %psum.69 = f32[4,4,512]{0,1,2:T(4,128)S(1)} all-reduce(f32[4,4,512]{0,1,2:T(4,128)S(1)} %broadcast_multiply_fusion.2), channel_id=1, replica_groups=mesh['group'=2,'chan'=16] {'chan'}, use_global_device_ids=true, to_apply=%region_6.0 | all-reduce | flops 8192 | bytes 65536 | tf_op jit(solution)/shard_map/psum | solution.py:108
  484.4 3.5 convolution_bitcast_fusion.2
  489.7 69.2 %psum.70 = f32[4,4,512]{0,1,2:T(4,128)S(1)} all-reduce(f32[4,4,512]{0,1,2:T(4,128)S(1)} %broadcast_multiply_fusion.1), channel_id=1, replica_groups=mesh['group'=2,'chan'=16] {'chan'}, use_global_device_ids=true, to_apply=%region_7.0 | all-reduce | flops 8192 | bytes 65536 | tf_op jit(solution)/shard_map/psum | solution.py:108
  558.9 3.5 convolution_bitcast_fusion.1
  564.2 69.3 %psum.71 = f32[4,4,512]{0,1,2:T(4,128)S(1)} all-reduce(f32[4,4,512]{0,1,2:T(4,128)S(1)} %broadcast_multiply_fusion), channel_id=1, replica_groups=mesh['group'=2,'chan'=16] {'chan'}, use_global_device_ids=true, to_apply=%region_8.0 | all-reduce | flops 8192 | bytes 65536 | tf_op jit(solution)/shard_map/psum | solution.py:108
  633.6 3.5 convolution_bitcast_fusion
  638.1 8.8 %fusion.80 = (bf16[1024,512]{1,0:T(8,128)(2,1)S(1)}, bf16[1024,512]{1,0:T(8,128)(2,1)S(1)}) fusion(f32[512]{0:T(512)S(1)} %bitcast.311, f32[]{:T(128)S(6)} %mul_shard_map.8, f32[512]{0:T(512)S(1)} %bitcast.315, f32[1024]{0:T(1024)S(1)} %bitcast.302, f32[512]{0:T(512)S(1)} %bitcast.313, f32[1024]{0:T(1024)S(1)} %bitcast.300, f32[512]{0:T(512)S(1)} %bitcast.305, ...), kind=kLoop, calls=%fused_computation.196 | loop fusion | flops 10485760 | bytes 2117636 | tf_op jit(solution)/shard_map/neg | solution.py:62
  646.9 9.4 %negate_convert_fusion.1 = (bf16[1024,512]{1,0:T(8,128)(2,1)S(1)}, bf16[1024,512]{1,0:T(8,128)(2,1)S(1)}, bf16[1024,512]{1,0:T(8,128)(2,1)S(1)}, bf16[1024,512]{1,0:T(8,128)(2,1)S(1)}) fusion(f32[]{:T(128)S(6)} %mul_shard_map.8, f32[512]{0:T(512)S(1)} %bitcast.312, f32[512]{0:T(512)S(1)} %bitcast.316, f32[1024]{0:T(1024)S(1)} %bitcast.303, ...), kind=kLoop, calls=%fused_computation.6 | loop fusion | flops 11534336 | bytes 4214788 | tf_op jit(solution)/shard_map/convert_element_type | solution.py:61
  656.3 1.5 fusion.7
  657.8 1.5 fusion.6
  659.3 1.5 fusion.4
  660.8 1.5 fusion.5
  665.1 3.5 all-to-all-start
  670.9 5.6 all-to-all-done
  676.5 3.5 all-to-all-start.1
  681.4 6.4 all-to-all-done.1
  688.8 1.3 copy.102
  (90 shorter events, 22.5 us)
Async XLA Ops:
  7.2 4.9 copy-start
  7.2 101.6 %all-reduce.3.cloned.1.call-start = ((), (), s32[]{:S(2)}) async-start(), calls=%async_computation.2 | async-start | bytes 2162688 | tf_op jit(solution)/shard_map/psum | solution.py:105
  10.3 1.7 copy-start.4
  10.4 1.7 copy-start.6
  108.7 1.6 copy-start.1
  113.9 1.0 copy-start.2
  637.1 1.0 copy-start.3
  646.9 9.4 %copy-start.5 = (bf16[1,2,256,1024]{3,2,1,0:T(8,128)(2,1)S(1)}, bf16[1,2,256,1024]{3,2,1,0:T(8,128)(2,1)}, u32[]{:S(2)}) copy-start(bf16[1,2,256,1024]{3,2,1,0:T(8,128)(2,1)} %param.7) | copy-start | bytes 3145732
  665.1 11.4 %all-to-all-start = ((bf16[16,2,2048]{2,1,0:T(2,128)(2,1)}), bf16[16,2,2048]{2,1,0:T(2,128)(2,1)S(1)}, u32[]{:S(2)}, u32[]{:S(2)}) async-start(bf16[16,2,2048]{2,1,0:T(2,128)(2,1)} %reshape.2137), calls=%async_computation | async-start | bytes 262144 | tf_op jit(solution)/shard_map/all_to_all | solution.py:127
  676.5 11.4 %all-to-all-start.1 = ((bf16[16,2,2048]{2,1,0:T(2,128)(2,1)}), bf16[16,2,2048]{2,1,0:T(2,128)(2,1)S(1)}, u32[]{:S(2)}, u32[]{:S(2)}) async-start(bf16[16,2,2048]{2,1,0:T(2,128)(2,1)} %reshape.2135), calls=%async_computation.1 | async-start | bytes 262144 | tf_op jit(solution)/shard_map/all_to_all | solution.py:127
Sparse Core Ops, SparseCore 0:
  12.1 96.5 all-reduce.2
where the time goes:
time: 704 us; the launch traced here: 697 us
  blocking collectives  486 us (69%)
  waiting for transfers between devices  107 us (15%)
  matrix products  43.8 us (6%)
  other arithmetic  29.8 us (4%)
  between operations  15 us (2%)
  local copies, waits for them, and re-layouts  9.1 us (1%)
  starting transfers between devices  7.06 us (1%)
    psum x7, blocking collectives, body(): summed = lax.psum(numerator, 'chan')  486 us
    psum x1, waiting for transfers between devices, body(): gram_all, summed = lax.psum((gram, numerator), 'chan')  94.6 us
    dot_general x8, matrix products, body(): jnp.einsum('kjs,jqs->kqs', inverse, summed, precision=HIGHEST)  28.4 us
  transfers between devices with their start and end apart: 3, of which 3 were waited for; matrix products, arithmetic and copies ran while one was open for 1% of the time, Pallas kernels for 0%

commit v1 on v0

--- a/solution.py
+++ b/solution.py
@@ -105,7 +105,8 @@
             gram_all, summed = lax.psum((gram, numerator), "chan")
             inverse = invert_small(gram_all + RIDGE * identity)
         else:
-            summed = lax.psum(numerator, "chan")
+            parts = lax.all_gather(numerator, "chan")
+            summed = jnp.sum(parts, axis=0)
         coefficients = jnp.einsum("kjs,jqs->kqs", inverse, summed, precision=HIGHEST)
         fitted = jnp.einsum("ck,kqs->cqs", basis, coefficients, precision=HIGHEST)
         dual = dual + mask * (local - fitted)

time: 704 us -> 350 us (0.50)
  blocking collectives: 486 us -> 142 us
  waiting for transfers between devices: 107 us -> 98.8 us
    psum x7 -> x0, blocking collectives: 486 us -> none  [body(): summed = lax.psum(numerator, 'chan')]
    all_gather x0 -> x7, blocking collectives: none -> 142 us  [body(): parts = lax.all_gather(numerator, 'chan')]
    psum x1, waiting for transfers between devices: 94.6 us -> 86.8 us  [body(): gram_all, summed = lax.psum((gram, numerator), 'chan')]
  transfers between devices with their start and end apart: 3 -> 3, of which waited for: 3 -> 3; matrix products, arithmetic and copies ran while one was open for 1% -> 2% of each run, Pallas kernels for 0% -> 0%
where the time goes in v1:
time: 350 us; the launch traced here: 344 us
  blocking collectives  142 us (41%)
  waiting for transfers between devices  98.8 us (28%)
  matrix products  44.5 us (13%)
  other arithmetic  25.6 us (7%)
  between operations  14.8 us (4%)
  local copies, waits for them, and re-layouts  12 us (3%)
  starting transfers between devices  7.06 us (2%)
    all_gather x7, blocking collectives, body(): parts = lax.all_gather(numerator, 'chan')  142 us
    psum x1, waiting for transfers between devices, body(): gram_all, summed = lax.psum((gram, numerator), 'chan')  86.8 us
    dot_general x8, matrix products, body(): jnp.einsum('kjs,jqs->kqs', inverse, summed, precision=HIGHEST)  28.4 us
    all_to_all x2, waiting for transfers between devices, body(): lax.all_to_all(average_pairs(jnp.stack(powers, axis=1)), 'chan', split_ax...  12 us
    convert_element_type x1, other arithmetic, beam_matrices(): w_im = (-(gain_re * sine + gain_im * cosine)).astype(jnp.bfloat16)  9.18 us
    neg x1, other arithmetic, beam_matrices(): upper = jnp.concatenate([w_re, -w_im], axis=1)  8.97 us
    dot_general x8, matrix products, body(): fitted = jnp.einsum('ck,kqs->cqs', basis, coefficients, precision=HIGHEST)  7.55 us
    all_to_all x2, starting transfers between devices, body(): lax.all_to_all(average_pairs(jnp.stack(powers, axis=1)), 'chan', split_ax...  7.02 us
  transfers between devices with their start and end apart: 3, of which 3 were waited for; matrix products, arithmetic and copies ran while one was open for 2% of the time, Pallas kernels for 0%

profile of v1, /device:TPU:0, one launch (start us, length us, event | category | flops | bytes accessed | tf_op | source)
XLA Modules:
  0.0 344.4 jit_solution(4167736684230929887)
XLA Ops:
  11.7 2.7 fusion
  14.5 86.8 %all-reduce.3.cloned.1.call-done = (f32[4,4,512]{2,1,0:T(4,128)}, f32[4,4,512]{2,1,0:T(4,128)}) async-done(((f32[4,4,512]{2,1,0:T(4,128)}, f32[4,4,512]{2,1,0:T(4,128)}), (f32[4,4,512]{2,1,0:T(4,128)}, f32[4,4,512]{2,1,0:T(4,128)})) %all-reduce.3.cloned.1.call-update) | async-done | bytes 65552 | tf_op jit(solution)/shard_map/psum | solution.py:105
  103.2 3.5 %convolution_bitcast_fusion.7 = f32[4,4,512]{0,1,2:T(4,128)S(1)} fusion(f32[4,4,512]{0,1,2:T(4,128)S(1)} %copy.131, f32[4,4,512]{1,0,2:T(4,128)S(1)} %copy.132), kind=kOutput, calls=%fused_computation.19 | convolution fusion | flops 393216 | bytes 98304 | tf_op jit(solution)/shard_map/kjs,jqs->kqs/dot_general | solution.py:110
  107.8 23.6 %all-gather = f32[64,4,512]{2,1,0:T(4,128)S(1)} all-gather(f32[4,4,512]{2,1,0:T(4,128)S(1)} %broadcast_multiply_fusion.6), channel_id=2, replica_groups=mesh['group'=2,'chan'=16] {'chan'}, dimensions={0}, use_global_device_ids=true | all-gather | bytes 557056 | tf_op jit(solution)/shard_map/all_gather | solution.py:108
  132.0 3.5 %convolution_bitcast_fusion.6 = f32[4,4,512]{0,1,2:T(4,128)S(1)} fusion(f32[4,4,512]{0,1,2:T(4,128)S(1)} %copy.133, f32[4,4,512]{1,0,2:T(4,128)S(1)} %copy.132), kind=kOutput, calls=%fused_computation.18 | convolution fusion | flops 393216 | bytes 98304 | tf_op jit(solution)/shard_map/kjs,jqs->kqs/dot_general | solution.py:110
  135.5 0.9 fusion.20
  136.6 18.9 %all-gather.1 = f32[64,4,512]{2,1,0:T(4,128)S(1)} all-gather(f32[4,4,512]{2,1,0:T(4,128)S(1)} %broadcast_multiply_fusion.5), channel_id=3, replica_groups=mesh['group'=2,'chan'=16] {'chan'}, dimensions={0}, use_global_device_ids=true | all-gather | bytes 557056 | tf_op jit(solution)/shard_map/all_gather | solution.py:108
  156.0 3.5 %convolution_bitcast_fusion.5 = f32[4,4,512]{0,1,2:T(4,128)S(1)} fusion(f32[4,4,512]{0,1,2:T(4,128)S(1)} %copy.135, f32[4,4,512]{1,0,2:T(4,128)S(1)} %copy.132), kind=kOutput, calls=%fused_computation.17 | convolution fusion | flops 393216 | bytes 98304 | tf_op jit(solution)/shard_map/kjs,jqs->kqs/dot_general | solution.py:110
  159.5 0.9 fusion.18
  160.6 20.5 %all-gather.2 = f32[64,4,512]{2,1,0:T(4,128)S(1)} all-gather(f32[4,4,512]{2,1,0:T(4,128)S(1)} %broadcast_multiply_fusion.4), channel_id=4, replica_groups=mesh['group'=2,'chan'=16] {'chan'}, dimensions={0}, use_global_device_ids=true | all-gather | bytes 557056 | tf_op jit(solution)/shard_map/all_gather | solution.py:108
  181.6 3.5 %convolution_bitcast_fusion.4 = f32[4,4,512]{0,1,2:T(4,128)S(1)} fusion(f32[4,4,512]{0,1,2:T(4,128)S(1)} %copy.137, f32[4,4,512]{1,0,2:T(4,128)S(1)} %copy.132), kind=kOutput, calls=%fused_computation.16 | convolution fusion | flops 393216 | bytes 98304 | tf_op jit(solution)/shard_map/kjs,jqs->kqs/dot_general | solution.py:110
  185.2 0.9 fusion.16
  186.3 18.9 %all-gather.3 = f32[64,4,512]{2,1,0:T(4,128)S(1)} all-gather(f32[4,4,512]{2,1,0:T(4,128)S(1)} %broadcast_multiply_fusion.3), channel_id=5, replica_groups=mesh['group'=2,'chan'=16] {'chan'}, dimensions={0}, use_global_device_ids=true | all-gather | bytes 557056 | tf_op jit(solution)/shard_map/all_gather | solution.py:108
  205.6 3.5 %convolution_bitcast_fusion.3 = f32[4,4,512]{0,1,2:T(4,128)S(1)} fusion(f32[4,4,512]{0,1,2:T(4,128)S(1)} %copy.139, f32[4,4,512]{1,0,2:T(4,128)S(1)} %copy.132), kind=kOutput, calls=%fused_computation.15 | convolution fusion | flops 393216 | bytes 98304 | tf_op jit(solution)/shard_map/kjs,jqs->kqs/dot_general | solution.py:110
  209.2 0.9 fusion.14
  210.3 20.7 %all-gather.4 = f32[64,4,512]{2,1,0:T(4,128)S(1)} all-gather(f32[4,4,512]{2,1,0:T(4,128)S(1)} %broadcast_multiply_fusion.2), channel_id=6, replica_groups=mesh['group'=2,'chan'=16] {'chan'}, dimensions={0}, use_global_device_ids=true | all-gather | bytes 557056 | tf_op jit(solution)/shard_map/all_gather | solution.py:108
  231.5 3.5 %convolution_bitcast_fusion.2 = f32[4,4,512]{0,1,2:T(4,128)S(1)} fusion(f32[4,4,512]{0,1,2:T(4,128)S(1)} %copy.141, f32[4,4,512]{1,0,2:T(4,128)S(1)} %copy.132), kind=kOutput, calls=%fused_computation.14 | convolution fusion | flops 393216 | bytes 98304 | tf_op jit(solution)/shard_map/kjs,jqs->kqs/dot_general | solution.py:110
  236.1 18.9 %all-gather.5 = f32[64,4,512]{2,1,0:T(4,128)S(1)} all-gather(f32[4,4,512]{2,1,0:T(4,128)S(1)} %broadcast_multiply_fusion.1), channel_id=7, replica_groups=mesh['group'=2,'chan'=16] {'chan'}, dimensions={0}, use_global_device_ids=true | all-gather | bytes 557056 | tf_op jit(solution)/shard_map/all_gather | solution.py:108
  255.5 3.5 %convolution_bitcast_fusion.1 = f32[4,4,512]{0,1,2:T(4,128)S(1)} fusion(f32[4,4,512]{0,1,2:T(4,128)S(1)} %copy.143, f32[4,4,512]{1,0,2:T(4,128)S(1)} %copy.132), kind=kOutput, calls=%fused_computation.13 | convolution fusion | flops 393216 | bytes 98304 | tf_op jit(solution)/shard_map/kjs,jqs->kqs/dot_general | solution.py:110
  260.1 20.3 %all-gather.6 = f32[64,4,512]{2,1,0:T(4,128)S(1)} all-gather(f32[4,4,512]{2,1,0:T(4,128)S(1)} %broadcast_multiply_fusion), channel_id=8, replica_groups=mesh['group'=2,'chan'=16] {'chan'}, dimensions={0}, use_global_device_ids=true | all-gather | bytes 557056 | tf_op jit(solution)/shard_map/all_gather | solution.py:108
  280.9 3.5 %convolution_bitcast_fusion = f32[4,4,512]{0,1,2:T(4,128)S(1)} fusion(f32[4,4,512]{0,1,2:T(4,128)S(1)} %copy.145, f32[4,4,512]{1,0,2:T(4,128)S(1)} %copy.132), kind=kOutput, calls=%fused_computation.12 | convolution fusion | flops 393216 | bytes 98304 | tf_op jit(solution)/shard_map/kjs,jqs->kqs/dot_general | solution.py:110
  285.5 9.0 %fusion.80 = (bf16[1024,512]{1,0:T(8,128)(2,1)S(1)}, bf16[1024,512]{1,0:T(8,128)(2,1)S(1)}) fusion(f32[512]{0:T(512)S(1)} %bitcast.325, f32[]{:T(128)S(6)} %mul_shard_map.8, f32[512]{0:T(512)S(1)} %bitcast.329, f32[1024]{0:T(1024)S(1)} %bitcast.316, f32[512]{0:T(512)S(1)} %bitcast.327, f32[1024]{0:T(1024)S(1)} %bitcast.314, f32[512]{0:T(512)S(1)} %bitcast.319, ...), kind=kLoop, calls=%fused_computation.196 | loop fusion | flops 10485760 | bytes 2117636 | tf_op jit(solution)/shard_map/neg | solution.py:62
  294.4 9.2 %negate_convert_fusion.1 = (bf16[1024,512]{1,0:T(8,128)(2,1)S(1)}, bf16[1024,512]{1,0:T(8,128)(2,1)S(1)}, bf16[1024,512]{1,0:T(8,128)(2,1)S(1)}, bf16[1024,512]{1,0:T(8,128)(2,1)S(1)}) fusion(f32[]{:T(128)S(6)} %mul_shard_map.8, f32[512]{0:T(512)S(1)} %bitcast.326, f32[512]{0:T(512)S(1)} %bitcast.330, f32[1024]{0:T(1024)S(1)} %bitcast.317, ...), kind=kLoop, calls=%fused_computation.6 | loop fusion | flops 11534336 | bytes 4214788 | tf_op jit(solution)/shard_map/convert_element_type | solution.py:61
  303.6 1.5 fusion.7
  305.1 1.5 fusion.6
  306.6 1.5 fusion.4
  308.1 1.5 fusion.5
  312.4 3.5 %all-to-all-start = ((bf16[16,2,2048]{2,1,0:T(2,128)(2,1)}), bf16[16,2,2048]{2,1,0:T(2,128)(2,1)S(1)}, u32[]{:S(2)}, u32[]{:S(2)}) async-start(bf16[16,2,2048]{2,1,0:T(2,128)(2,1)} %reshape.2144), calls=%async_computation | async-start | bytes 262144 | tf_op jit(solution)/shard_map/all_to_all | solution.py:128
  318.2 5.6 %all-to-all-done = bf16[16,2,2048]{2,1,0:T(2,128)(2,1)S(1)} async-done(((bf16[16,2,2048]{2,1,0:T(2,128)(2,1)}), bf16[16,2,2048]{2,1,0:T(2,128)(2,1)S(1)}, u32[]{:S(2)}, u32[]{:S(2)}) %all-to-all-start) | async-done | bytes 131104 | tf_op jit(solution)/shard_map/all_to_all | solution.py:128
  323.7 3.5 %all-to-all-start.1 = ((bf16[16,2,2048]{2,1,0:T(2,128)(2,1)}), bf16[16,2,2048]{2,1,0:T(2,128)(2,1)S(1)}, u32[]{:S(2)}, u32[]{:S(2)}) async-start(bf16[16,2,2048]{2,1,0:T(2,128)(2,1)} %reshape.2142), calls=%async_computation.1 | async-start | bytes 262144 | tf_op jit(solution)/shard_map/all_to_all | solution.py:128
  328.7 6.4 %all-to-all-done.1 = bf16[16,2,2048]{2,1,0:T(2,128)(2,1)S(1)} async-done(((bf16[16,2,2048]{2,1,0:T(2,128)(2,1)}), bf16[16,2,2048]{2,1,0:T(2,128)(2,1)S(1)}, u32[]{:S(2)}, u32[]{:S(2)}) %all-to-all-start.1) | async-done | bytes 131104 | tf_op jit(solution)/shard_map/all_to_all | solution.py:128
  336.1 1.3 copy.151
  (93 shorter events, 22.0 us)
Async XLA Ops:
  7.2 4.5 %copy-start = (f32[2,1024]{1,0:T(2,128)S(1)}, f32[2,1024]{1,0:T(2,128)}, u32[]{:S(2)}) copy-start(f32[2,1024]{1,0:T(2,128)} %param.12) | copy-start | bytes 24580
  7.2 94.0 %all-reduce.3.cloned.1.call-start = ((), (), s32[]{:S(2)}) async-start(), calls=%async_computation.2 | async-start | bytes 131072 | tf_op jit(solution)/shard_map/psum | solution.py:105
  101.2 1.6 copy-start.2
  106.8 1.0 copy-start.1
  284.5 1.0 copy-start.3
  294.4 9.2 %copy-start.4 = (bf16[1,2,256,1024]{3,2,1,0:T(8,128)(2,1)S(1)}, bf16[1,2,256,1024]{3,2,1,0:T(8,128)(2,1)}, u32[]{:S(2)}) copy-start(bf16[1,2,256,1024]{3,2,1,0:T(8,128)(2,1)} %param.7) | copy-start | bytes 3145732
  312.4 11.4 %all-to-all-start = ((bf16[16,2,2048]{2,1,0:T(2,128)(2,1)}), bf16[16,2,2048]{2,1,0:T(2,128)(2,1)S(1)}, u32[]{:S(2)}, u32[]{:S(2)}) async-start(bf16[16,2,2048]{2,1,0:T(2,128)(2,1)} %reshape.2144), calls=%async_computation | async-start | bytes 262144 | tf_op jit(solution)/shard_map/all_to_all | solution.py:128
  323.7 11.4 %all-to-all-start.1 = ((bf16[16,2,2048]{2,1,0:T(2,128)(2,1)}), bf16[16,2,2048]{2,1,0:T(2,128)(2,1)S(1)}, u32[]{:S(2)}, u32[]{:S(2)}) async-start(bf16[16,2,2048]{2,1,0:T(2,128)(2,1)} %reshape.2142), calls=%async_computation.1 | async-start | bytes 262144 | tf_op jit(solution)/shard_map/all_to_all | solution.py:128
Sparse Core Ops, SparseCore 0:
  12.1 89.0 all-reduce.2
